TPU v7x, 128 devices: a whole 4x4x4 slice. The times are simulated.
128 devices in a mesh: row: 16 (over y, x), col: 8 (over z, core).
Axes of the slice: x: 4, y: 4, z: 4, core: 2. Of those that a mesh axis runs over, the one named last changes fastest.
Arguments:
- x_blocks: bfloat16 [128, 16, 256, 256], P('row', 'col'), may hold values from -0.75 to 0.75, as said below
- x_cols: int32 [128, 16], P('row', 'col'), may hold values from -1 to 127, as said below
- out_cols: int32 [128, 32], P('row', 'col'), may hold values from 0 to 127, as said below
- branch_flag: int32 [128], P('row'), may hold values from 0 to 1
Outputs:
- purified: bfloat16 [128, 32, 256, 256], P('row', 'col')
- trace: float32 [1], replicated
Inputs may be any that keep to these rules, and one draw needn't show every extreme that they name: `x_cols`: slot c * 2 + s of block row i holds -1 or a block column in c * 16 to (c + 1) * 16 - 1; the filled columns of one block row are distinct. The pattern is symmetric: block row i names column j exactly when block row j names column i. The rows of one device hold at most 13 filled slots together, and the rows of some device hold exactly 13. `x_blocks`: the stored block of position (j, i) is the transpose of the stored block of position (i, j); stored diagonal blocks are symmetric. `out_cols`: slot c * 4 + o of block row i holds a block column in c * 16 to (c + 1) * 16 - 1, distinct within one block row; column i is always among the slots of block row i. `branch_flag`: entry i is 0 where block row i takes X times X, 1 where it takes 2 X minus X times X.
All inputs are finite; a program needn't handle non-finite values.
Results may differ from a plain program's by a relative error of at most 0.001.
Values may be sent and summed in bfloat16 or wider, within the bound.
A program may use at most 192 MiB of HBM per device.

v0:
```python
import jax
import jax.numpy as jnp
from jax import lax
from jax.sharding import PartitionSpec as P


def per_device(x_blocks, x_cols, out_cols, branch_flag):
    rows = x_cols.shape[0]
    slots = x_cols.shape[1]
    block = x_blocks.shape[-1]
    kept = out_cols.shape[1]
    filled = x_cols >= 0
    cleared = jnp.where(filled[:, :, None, None], x_blocks, jnp.zeros_like(x_blocks))
    flag_rows = branch_flag == 1
    base_row = lax.axis_index("row") * rows
    left_blocks, left_cols = (
        lax.all_gather(cleared, "col", axis=1, tiled=True),
        lax.all_gather(x_cols, "col", axis=1, tiled=True),
    )
    right_blocks, right_cols = (
        lax.all_gather(cleared, "row", axis=0, tiled=True),
        lax.all_gather(x_cols, "row", axis=0, tiled=True),
    )

    def fetch(local):
        entries = left_cols[local]
        live = entries >= 0
        source_rows = jnp.where(live, entries, 0)
        fetched = right_blocks[source_rows]
        fetched_cols = jnp.where(live[:, None], right_cols[source_rows], -1)
        return (left_blocks[local], fetched, fetched_cols)

    def one_row(local):
        lhs, fetched, fetched_cols = fetch(local)
        width = fetched_cols.shape[0] * fetched_cols.shape[1]
        products = jnp.einsum("exy,esyz->esxz", lhs, fetched, preferred_element_type=jnp.float32)
        targets = out_cols[local]
        match = (
            (fetched_cols[None, :, :] == targets[:, None, None])
            .astype(jnp.float32)
            .reshape(kept, width)
        )
        square = jnp.dot(
            match, products.reshape(width, block * block), precision=lax.Precision.HIGHEST
        ).reshape(kept, block, block)
        own_match = (x_cols[local][None, :] == targets[:, None]).astype(jnp.float32)
        own_blocks = cleared[local].astype(jnp.float32).reshape(slots, block * block)
        own = jnp.dot(own_match, own_blocks, precision=lax.Precision.HIGHEST).reshape(
            kept, block, block
        )
        result = jnp.where(flag_rows[local], 2.0 * own - square, square)
        diag_here = (targets == base_row + local).astype(jnp.float32)
        part = jnp.sum(diag_here * jnp.trace(result, axis1=1, axis2=2))
        return (result.astype(jnp.bfloat16), part)

    purified, parts = lax.map(one_row, jnp.arange(rows, dtype=jnp.int32))
    trace_total = lax.psum(jnp.sum(parts), ("row", "col"))
    return (purified, trace_total.reshape(1))


def solution(mesh):
    in_specs = (P("row", "col", None, None), P("row", "col"), P("row", "col"), P("row"))
    out_specs = (P("row", "col", None, None), P())
    return jax.shard_map(
        per_device, mesh=mesh, in_specs=in_specs, out_specs=out_specs, check_vma=False
    )
```

profile of v0, /device:TPU:1, one launch (start us, length us, event | category | flops | bytes accessed | tf_op | source)
XLA Modules:
  0.0 680.2 jit_solution(9202901547140222061)
XLA Ops:
  8.0 3.2 broadcast_select_fusion.1
  12.0 19.4 %all-gather.1 = s32[16,8,2]{1,2,0:T(2,128)S(1)} all-gather(s32[1,8,2]{1,2,0:T(2,128)S(1)} %bitcast.109), channel_id=1, replica_groups=mesh['row'=16,'col'=8] {'row'}, dimensions={0}, use_global_device_ids=true | all-gather | bytes 1088 | tf_op jit(solution)/shard_map/all_gather | solution.py:22
  31.6 17.7 %all-gather = s32[8,2,8]{2,1,0:T(2,128)S(1)} all-gather(s32[1,2,8]{2,1,0:T(2,128)S(1)} %bitcast.110), channel_id=1, replica_groups=mesh['row'=16,'col'=8] {'col'}, dimensions={0}, use_global_device_ids=true | all-gather | bytes 576 | tf_op jit(solution)/shard_map/all_gather | solution.py:18
  49.5 50.6 %all-gather.7.cloned.1.call-done = bf16[8,16,256,256]{3,2,1,0:T(8,128)(2,1)} async-done(((bf16[8,2,256,256]{3,2,1,0:T(8,128)(2,1)}), bf16[8,16,256,256]{3,2,1,0:T(8,128)(2,1)}) %all-gather.7.cloned.1.call-update) | async-done | bytes 16777232 | tf_op jit(solution)/shard_map/all_gather | solution.py:17
  100.1 198.9 %all-gather.5.cloned.1.call-done = bf16[128,2,256,256]{3,2,1,0:T(8,128)(2,1)} async-done(((bf16[8,2,256,256]{3,2,1,0:T(8,128)(2,1)}), bf16[128,2,256,256]{3,2,1,0:T(8,128)(2,1)}) %all-gather.5.cloned.1.call-update) | async-done | bytes 33554448 | tf_op jit(solution)/shard_map/all_gather | solution.py:21
  299.0 307.8 %while.12 = (s32[]{:T(128)}, bf16[8,4,256,256]{3,2,1,0:T(8,128)(2,1)}, f32[8]{0:T(128)S(1)}, s32[8]{0:T(128)S(1)}, pred[8]{0:T(512)(128)(4,1)S(1)}, /*index=5*/s...) while((s32[]{:T(128)}, ...), condition=%wide.region_3.4_spmd, body=%wide.region_0.3_spmd.sunk | while | flops 1177093376 | bytes 52828456 | solution.py:56
  301.5 4.9 gather_fusion.1
  306.4 7.4 %convolution_bitcast_fusion.2 = f32[16,2,256,256]{2,3,1,0:T(8,128)} fusion(bf16[16,2,256,256]{3,2,1,0:T(8,128)(2,1)} %gather_fusion.1, bf16[8,16,256,256]{3,2,1,0:T(8,128)(2,1)} %get-tuple-element.271, s32[]{:T(128)S(6)} %select_n.86), kind=kOutput, calls=%fused_computation.5.clone.1 | convolution fusion | flops 1073741824 | bytes 14680068 | tf_op jit(solution)/shard_map/while/body/eval_jaxpr/exy,esyz->esxz/dot_general | solution.py:36
  313.8 10.2 %copy.58 = f32[4,8,256,256]{3,1,2,0:T(8,128)} copy(f32[4,8,256,256]{2,3,1,0:T(8,128)} %bitcast.106) | data formatting | bytes 16777216 | tf_op jit(solution)/shard_map/while
  324.9 6.1 fusion.45
  331.0 1.0 dynamic-slice_bitcast_fusion.2
  332.7 1.8 select_reduce_fusion.2
  339.8 4.9 gather_fusion.1
  344.7 7.4 %convolution_bitcast_fusion.2 = f32[16,2,256,256]{2,3,1,0:T(8,128)} fusion(bf16[16,2,256,256]{3,2,1,0:T(8,128)(2,1)} %gather_fusion.1, bf16[8,16,256,256]{3,2,1,0:T(8,128)(2,1)} %get-tuple-element.271, s32[]{:T(128)S(6)} %select_n.86), kind=kOutput, calls=%fused_computation.5.clone.1 | convolution fusion | flops 1073741824 | bytes 14680068 | tf_op jit(solution)/shard_map/while/body/eval_jaxpr/exy,esyz->esxz/dot_general | solution.py:36
  352.1 10.2 %copy.58 = f32[4,8,256,256]{3,1,2,0:T(8,128)} copy(f32[4,8,256,256]{2,3,1,0:T(8,128)} %bitcast.106) | data formatting | bytes 16777216 | tf_op jit(solution)/shard_map/while
  363.2 6.1 fusion.45
  371.0 1.8 select_reduce_fusion.2
  378.1 4.9 gather_fusion.1
  383.0 7.4 %convolution_bitcast_fusion.2 = f32[16,2,256,256]{2,3,1,0:T(8,128)} fusion(bf16[16,2,256,256]{3,2,1,0:T(8,128)(2,1)} %gather_fusion.1, bf16[8,16,256,256]{3,2,1,0:T(8,128)(2,1)} %get-tuple-element.271, s32[]{:T(128)S(6)} %select_n.86), kind=kOutput, calls=%fused_computation.5.clone.1 | convolution fusion | flops 1073741824 | bytes 14680068 | tf_op jit(solution)/shard_map/while/body/eval_jaxpr/exy,esyz->esxz/dot_general | solution.py:36
  390.4 10.2 %copy.58 = f32[4,8,256,256]{3,1,2,0:T(8,128)} copy(f32[4,8,256,256]{2,3,1,0:T(8,128)} %bitcast.106) | data formatting | bytes 16777216 | tf_op jit(solution)/shard_map/while
  401.6 6.1 fusion.45
  409.3 1.8 select_reduce_fusion.2
  416.5 5.4 gather_fusion.1
  421.8 7.4 %convolution_bitcast_fusion.2 = f32[16,2,256,256]{2,3,1,0:T(8,128)} fusion(bf16[16,2,256,256]{3,2,1,0:T(8,128)(2,1)} %gather_fusion.1, bf16[8,16,256,256]{3,2,1,0:T(8,128)(2,1)} %get-tuple-element.271, s32[]{:T(128)S(6)} %select_n.86), kind=kOutput, calls=%fused_computation.5.clone.1 | convolution fusion | flops 1073741824 | bytes 14680068 | tf_op jit(solution)/shard_map/while/body/eval_jaxpr/exy,esyz->esxz/dot_general | solution.py:36
  429.3 10.2 %copy.58 = f32[4,8,256,256]{3,1,2,0:T(8,128)} copy(f32[4,8,256,256]{2,3,1,0:T(8,128)} %bitcast.106) | data formatting | bytes 16777216 | tf_op jit(solution)/shard_map/while
  440.4 6.1 fusion.45
  448.2 1.8 select_reduce_fusion.2
  455.3 4.9 gather_fusion.1
  460.2 7.4 %convolution_bitcast_fusion.2 = f32[16,2,256,256]{2,3,1,0:T(8,128)} fusion(bf16[16,2,256,256]{3,2,1,0:T(8,128)(2,1)} %gather_fusion.1, bf16[8,16,256,256]{3,2,1,0:T(8,128)(2,1)} %get-tuple-element.271, s32[]{:T(128)S(6)} %select_n.86), kind=kOutput, calls=%fused_computation.5.clone.1 | convolution fusion | flops 1073741824 | bytes 14680068 | tf_op jit(solution)/shard_map/while/body/eval_jaxpr/exy,esyz->esxz/dot_general | solution.py:36
  467.6 10.2 %copy.58 = f32[4,8,256,256]{3,1,2,0:T(8,128)} copy(f32[4,8,256,256]{2,3,1,0:T(8,128)} %bitcast.106) | data formatting | bytes 16777216 | tf_op jit(solution)/shard_map/while
  478.7 6.1 fusion.45
  486.5 1.8 select_reduce_fusion.2
  493.6 5.0 gather_fusion.1
  498.6 7.4 %convolution_bitcast_fusion.2 = f32[16,2,256,256]{2,3,1,0:T(8,128)} fusion(bf16[16,2,256,256]{3,2,1,0:T(8,128)(2,1)} %gather_fusion.1, bf16[8,16,256,256]{3,2,1,0:T(8,128)(2,1)} %get-tuple-element.271, s32[]{:T(128)S(6)} %select_n.86), kind=kOutput, calls=%fused_computation.5.clone.1 | convolution fusion | flops 1073741824 | bytes 14680068 | tf_op jit(solution)/shard_map/while/body/eval_jaxpr/exy,esyz->esxz/dot_general | solution.py:36
  506.1 10.2 %copy.58 = f32[4,8,256,256]{3,1,2,0:T(8,128)} copy(f32[4,8,256,256]{2,3,1,0:T(8,128)} %bitcast.106) | data formatting | bytes 16777216 | tf_op jit(solution)/shard_map/while
  517.2 6.1 fusion.45
  524.9 1.8 select_reduce_fusion.2
  532.1 5.0 gather_fusion.1
  537.1 7.4 %convolution_bitcast_fusion.2 = f32[16,2,256,256]{2,3,1,0:T(8,128)} fusion(bf16[16,2,256,256]{3,2,1,0:T(8,128)(2,1)} %gather_fusion.1, bf16[8,16,256,256]{3,2,1,0:T(8,128)(2,1)} %get-tuple-element.271, s32[]{:T(128)S(6)} %select_n.86), kind=kOutput, calls=%fused_computation.5.clone.1 | convolution fusion | flops 1073741824 | bytes 14680068 | tf_op jit(solution)/shard_map/while/body/eval_jaxpr/exy,esyz->esxz/dot_general | solution.py:36
  544.6 10.2 %copy.58 = f32[4,8,256,256]{3,1,2,0:T(8,128)} copy(f32[4,8,256,256]{2,3,1,0:T(8,128)} %bitcast.106) | data formatting | bytes 16777216 | tf_op jit(solution)/shard_map/while
  555.7 6.1 fusion.45
  563.4 1.8 select_reduce_fusion.2
  570.6 5.3 gather_fusion.1
  575.8 7.4 %convolution_bitcast_fusion.2 = f32[16,2,256,256]{2,3,1,0:T(8,128)} fusion(bf16[16,2,256,256]{3,2,1,0:T(8,128)(2,1)} %gather_fusion.1, bf16[8,16,256,256]{3,2,1,0:T(8,128)(2,1)} %get-tuple-element.271, s32[]{:T(128)S(6)} %select_n.86), kind=kOutput, calls=%fused_computation.5.clone.1 | convolution fusion | flops 1073741824 | bytes 14680068 | tf_op jit(solution)/shard_map/while/body/eval_jaxpr/exy,esyz->esxz/dot_general | solution.py:36
  583.3 10.2 %copy.58 = f32[4,8,256,256]{3,1,2,0:T(8,128)} copy(f32[4,8,256,256]{2,3,1,0:T(8,128)} %bitcast.106) | data formatting | bytes 16777216 | tf_op jit(solution)/shard_map/while
  594.4 6.1 fusion.45
  602.2 1.8 select_reduce_fusion.2
  607.4 66.0 %psum.7 = f32[1]{0:T(128)} all-reduce(f32[1]{0:T(128)} %bitcast.24), channel_id=1, replica_groups=mesh['row'=16,'col'=8] {'row','col'}, use_global_device_ids=true, to_apply=%region_5.6 | all-reduce | flops 1 | bytes 8 | tf_op jit(solution)/shard_map/psum | solution.py:57
  (156 shorter events, 44.0 us)
Async XLA Ops:
  7.2 93.0 %all-gather.7.cloned.1.call-start = ((), (), s32[]{:S(2)}) async-start(), calls=%async_computation.1 | async-start | bytes 18874368 | tf_op jit(solution)/shard_map/all_gather | solution.py:17
  8.0 4.0 copy-start
  8.0 41.4 %copy-start.1 = (s32[8,4]{0,1:T(4,128)S(1)}, s32[8,4]{0,1:T(4,128)}, u32[]{:S(2)}) copy-start(s32[8,4]{0,1:T(4,128)} %param.8) | copy-start | bytes 388
  8.0 41.5 %copy-start.2 = (s32[8]{0:T(128)S(1)}, s32[8]{0:T(128)}, u32[]{:S(2)}) copy-start(s32[8]{0:T(128)} %param.9) | copy-start | bytes 100
  11.2 287.8 %all-gather.5.cloned.1.call-start = ((), (), s32[]{:S(2)}) async-start(), calls=%async_computation | async-start | bytes 35651584 | tf_op jit(solution)/shard_map/all_gather | solution.py:21
Sparse Core Ops, SparseCore 0:
  11.3 88.7 all-gather.6
  102.3 196.6 all-gather.4
where the time goes:
time: 683 us; the launch traced here: 680 us
  waiting for transfers between devices  250 us (37%)
  local copies, waits for them, and re-layouts  159 us (23%)
  matrix products  123 us (18%)
  blocking collectives  103 us (15%)
  loops' own time  20.5 us (3%)
  between operations  14.1 us (2%)
  other arithmetic  10 us (1%)
    all_gather x1, waiting for transfers between devices, per_device(): lax.all_gather(cleared, 'row', axis=0, tiled=True)  199 us
    while x16, local copies, waits for them, and re-layouts  89.7 us
    psum x1, blocking collectives, per_device(): trace_total = lax.psum(jnp.sum(parts), ('row', 'col'))  66 us
    dot_general x8, matrix products, one_row(): jnp.einsum('exy,esyz->esxz', lhs, fetched, preferred_element_type=jnp.flo...  59.5 us
    all_gather x1, waiting for transfers between devices, per_device(): lax.all_gather(cleared, 'col', axis=1, tiled=True)  50.6 us
    dot_general x8, matrix products, one_row(): jnp.dot(match, products.reshape(width, block * block), precision=lax.Prec...  49 us
    gather x8, local copies, waits for them, and re-layouts, fetch(): fetched = right_blocks[source_rows]  40.2 us
    another operation x1, loops' own time, per_device(): purified, parts = lax.map(one_row, jnp.arange(rows, dtype=jnp.int32))  20.5 us
  transfers between devices with their start and end apart: 2, of which 2 were waited for; matrix products, arithmetic and copies ran while one was open for 0% of the time, Pallas kernels for 0%

commit v1 on v0

--- a/solution.py
+++ b/solution.py
@@ -2,6 +2,11 @@
 import jax.numpy as jnp
 from jax import lax
 from jax.sharding import PartitionSpec as P
+
+
+def gather_over(x, axis, along):
+    outgoing = jnp.stack([x] * lax.axis_size(axis))
+    return jnp.concatenate(lax.all_to_all(outgoing, axis, 0, 0), axis=along)
 
 
 def per_device(x_blocks, x_cols, out_cols, branch_flag):
@@ -14,7 +19,7 @@
     flag_rows = branch_flag == 1
     base_row = lax.axis_index("row") * rows
     left_blocks, left_cols = (
-        lax.all_gather(cleared, "col", axis=1, tiled=True),
+        gather_over(cleared, "col", 1),
         lax.all_gather(x_cols, "col", axis=1, tiled=True),
     )
     right_blocks, right_cols = (

time: 683 us -> 611 us (0.89)
  waiting for transfers between devices: 250 us -> 0.02 us
  blocking collectives: 103 us -> 254 us
  local copies, waits for them, and re-layouts: 159 us -> 180 us
  starting transfers between devices: 0.08 us -> 7.15 us
    all_gather x1, waiting for transfers between devices: 199 us -> 0.01 us  [per_device(): lax.all_gather(cleared, 'row', axis=0, tiled=True)]
    all_gather x1, blocking collectives: 17.7 us -> 166 us  [per_device(): lax.all_gather(x_cols, 'col', axis=1, tiled=True)]
    all_gather x1 -> x0, waiting for transfers between devices: 50.6 us -> none  [per_device(): lax.all_gather(cleared, 'col', axis=1, tiled=True)]
    all_to_all x0 -> x1, local copies, waits for them, and re-layouts: none -> 13.9 us  [gather_over(): return jnp.concatenate(lax.all_to_all(outgoing, axis, 0, 0), axis=along)]
    all_to_all x0 -> x1, starting transfers between devices: none -> 7.11 us  [gather_over(): return jnp.concatenate(lax.all_to_all(outgoing, axis, 0, 0), axis=along)]
    another operation x0 -> x1, local copies, waits for them, and re-layouts: none -> 6.84 us  [gather_over(): outgoing = jnp.stack([x] * lax.axis_size(axis))]
  transfers between devices with their start and end apart: 2 -> 2, of which waited for: 2 -> 0; matrix products, arithmetic and copies ran while one was open for 0% -> 3% of each run, Pallas kernels for 0% -> 0%
where the time goes in v1:
time: 611 us; the launch traced here: 608 us
  blocking collectives  254 us (42%)
  local copies, waits for them, and re-layouts  180 us (29%)
  matrix products  123 us (20%)
  loops' own time  20.5 us (3%)
  between operations  14 us (2%)
  other arithmetic  10 us (2%)
  starting transfers between devices  7.15 us (1%)
    all_gather x1, blocking collectives, per_device(): lax.all_gather(x_cols, 'col', axis=1, tiled=True)  166 us
    while x16, local copies, waits for them, and re-layouts  89.7 us
    psum x1, blocking collectives, per_device(): trace_total = lax.psum(jnp.sum(parts), ('row', 'col'))  66.4 us
    dot_general x8, matrix products, one_row(): jnp.einsum('exy,esyz->esxz', lhs, fetched, preferred_element_type=jnp.flo...  59.5 us
    dot_general x8, matrix products, one_row(): jnp.dot(match, products.reshape(width, block * block), precision=lax.Prec...  49 us
    gather x8, local copies, waits for them, and re-layouts, fetch(): fetched = right_blocks[source_rows]  40.2 us
    all_gather x1, blocking collectives, per_device(): lax.all_gather(x_cols, 'row', axis=0, tiled=True)  21.5 us
    another operation x1, loops' own time, per_device(): purified, parts = lax.map(one_row, jnp.arange(rows, dtype=jnp.int32))  20.5 us
  transfers between devices with their start and end apart: 2, of which 0 were waited for; matrix products, arithmetic and copies ran while one was open for 3% of the time, Pallas kernels for 0%

profile of v1, /device:TPU:1, one launch (start us, length us, event | category | flops | bytes accessed | tf_op | source)
XLA Modules:
  0.0 608.3 jit_solution(7083019634689144586)
XLA Ops:
  8.0 3.1 broadcast_select_fusion.1
  11.1 6.8 %stack.2 = bf16[8,8,2,256,256]{4,3,2,1,0:T(8,128)(2,1)} broadcast(bf16[8,2,256,256]{3,2,1,0:T(8,128)(2,1)} %broadcast_select_fusion.1), dimensions={1,2,3,4} | broadcast | bytes 18874368 | tf_op jit(solution)/shard_map/stack | solution.py:8
  18.0 7.1 %all-to-all-start = ((bf16[8,8,2,256,256]{4,3,2,1,0:T(8,128)(2,1)}), bf16[8,8,2,256,256]{4,3,2,1,0:T(8,128)(2,1)}, u32[]{:S(2)}, u32[]{:S(2)}) async-start(bf16[8,8,2,256,256]{4,3,2,1,0:T(8,128)(2,1)} %stack.2), calls=%async_computation | async-start | bytes 33554432 | tf_op jit(solution)/shard_map/all_to_all | solution.py:9
  25.2 21.5 %all-gather.1 = s32[16,8,2]{1,2,0:T(2,128)S(1)} all-gather(s32[1,8,2]{1,2,0:T(2,128)S(1)} %bitcast.113), channel_id=1, replica_groups=mesh['row'=16,'col'=8] {'row'}, dimensions={0}, use_global_device_ids=true | all-gather | bytes 1088 | tf_op jit(solution)/shard_map/all_gather | solution.py:27
  46.8 165.7 %all-gather = s32[8,2,8]{2,1,0:T(2,128)S(1)} all-gather(s32[1,2,8]{2,1,0:T(2,128)S(1)} %bitcast.114), channel_id=1, replica_groups=mesh['row'=16,'col'=8] {'col'}, dimensions={0}, use_global_device_ids=true | all-gather | bytes 576 | tf_op jit(solution)/shard_map/all_gather | solution.py:23
  212.7 13.9 %copy.37 = bf16[8,8,2,256,256]{4,3,2,0,1:T(8,128)(2,1)} copy(bf16[8,8,2,256,256]{4,3,2,1,0:T(8,128)(2,1)} %all-to-all-done) | data formatting | bytes 33554432 | tf_op jit(solution)/shard_map/all_to_all | solution.py:9
  226.6 307.8 %while.12 = (s32[]{:T(128)}, bf16[8,4,256,256]{3,2,1,0:T(8,128)(2,1)}, f32[8]{0:T(128)S(1)}, s32[8]{0:T(128)S(1)}, pred[8]{0:T(512)(128)(4,1)S(1)}, /*index=5*/s...) while((s32[]{:T(128)}, ...), condition=%wide.region_3.4_spmd, body=%wide.region_0.3_spmd.sunk | while | flops 1177093376 | bytes 52828456 | solution.py:61
  229.1 4.9 gather_fusion.1
  234.0 7.4 %convolution_bitcast_fusion.2 = f32[16,2,256,256]{2,3,1,0:T(8,128)} fusion(bf16[16,2,256,256]{3,2,1,0:T(8,128)(2,1)} %gather_fusion.1, bf16[8,16,256,256]{3,2,1,0:T(8,128)(2,1)} %get-tuple-element.286, s32[]{:T(128)S(6)} %select_n.86), kind=kOutput, calls=%fused_computation.5.clone.1 | convolution fusion | flops 1073741824 | bytes 14680068 | tf_op jit(solution)/shard_map/while/body/eval_jaxpr/exy,esyz->esxz/dot_general | solution.py:41
  241.4 10.2 %copy.69 = f32[4,8,256,256]{3,1,2,0:T(8,128)} copy(f32[4,8,256,256]{2,3,1,0:T(8,128)} %bitcast.109) | data formatting | bytes 16777216 | tf_op jit(solution)/shard_map/while
  252.5 6.1 %fusion.45 = f32[4,256,256]{2,0,1:T(4,128)S(1)} fusion(s32[32]{0:T(128)S(1)} %broadcast_select_fusion.3, s32[4]{0:T(128)S(1)} %fusion.44, f32[4,8,256,256]{3,1,2,0:T(8,128)} %copy.69), kind=kOutput, calls=%fused_computation.2.clone.1 | convolution fusion | flops 100663424 | bytes 9437328 | tf_op jit(solution)/shard_map/while/body/eval_jaxpr/dot_general | solution.py:48
  260.3 1.8 select_reduce_fusion.2
  267.4 4.9 gather_fusion.1
  272.3 7.4 %convolution_bitcast_fusion.2 = f32[16,2,256,256]{2,3,1,0:T(8,128)} fusion(bf16[16,2,256,256]{3,2,1,0:T(8,128)(2,1)} %gather_fusion.1, bf16[8,16,256,256]{3,2,1,0:T(8,128)(2,1)} %get-tuple-element.286, s32[]{:T(128)S(6)} %select_n.86), kind=kOutput, calls=%fused_computation.5.clone.1 | convolution fusion | flops 1073741824 | bytes 14680068 | tf_op jit(solution)/shard_map/while/body/eval_jaxpr/exy,esyz->esxz/dot_general | solution.py:41
  279.8 10.2 %copy.69 = f32[4,8,256,256]{3,1,2,0:T(8,128)} copy(f32[4,8,256,256]{2,3,1,0:T(8,128)} %bitcast.109) | data formatting | bytes 16777216 | tf_op jit(solution)/shard_map/while
  290.9 6.1 %fusion.45 = f32[4,256,256]{2,0,1:T(4,128)S(1)} fusion(s32[32]{0:T(128)S(1)} %broadcast_select_fusion.3, s32[4]{0:T(128)S(1)} %fusion.44, f32[4,8,256,256]{3,1,2,0:T(8,128)} %copy.69), kind=kOutput, calls=%fused_computation.2.clone.1 | convolution fusion | flops 100663424 | bytes 9437328 | tf_op jit(solution)/shard_map/while/body/eval_jaxpr/dot_general | solution.py:48
  298.6 1.8 select_reduce_fusion.2
  305.8 4.9 gather_fusion.1
  310.6 7.4 %convolution_bitcast_fusion.2 = f32[16,2,256,256]{2,3,1,0:T(8,128)} fusion(bf16[16,2,256,256]{3,2,1,0:T(8,128)(2,1)} %gather_fusion.1, bf16[8,16,256,256]{3,2,1,0:T(8,128)(2,1)} %get-tuple-element.286, s32[]{:T(128)S(6)} %select_n.86), kind=kOutput, calls=%fused_computation.5.clone.1 | convolution fusion | flops 1073741824 | bytes 14680068 | tf_op jit(solution)/shard_map/while/body/eval_jaxpr/exy,esyz->esxz/dot_general | solution.py:41
  318.1 10.2 %copy.69 = f32[4,8,256,256]{3,1,2,0:T(8,128)} copy(f32[4,8,256,256]{2,3,1,0:T(8,128)} %bitcast.109) | data formatting | bytes 16777216 | tf_op jit(solution)/shard_map/while
  329.2 6.1 %fusion.45 = f32[4,256,256]{2,0,1:T(4,128)S(1)} fusion(s32[32]{0:T(128)S(1)} %broadcast_select_fusion.3, s32[4]{0:T(128)S(1)} %fusion.44, f32[4,8,256,256]{3,1,2,0:T(8,128)} %copy.69), kind=kOutput, calls=%fused_computation.2.clone.1 | convolution fusion | flops 100663424 | bytes 9437328 | tf_op jit(solution)/shard_map/while/body/eval_jaxpr/dot_general | solution.py:48
  337.0 1.8 select_reduce_fusion.2
  344.1 5.4 gather_fusion.1
  349.5 7.4 %convolution_bitcast_fusion.2 = f32[16,2,256,256]{2,3,1,0:T(8,128)} fusion(bf16[16,2,256,256]{3,2,1,0:T(8,128)(2,1)} %gather_fusion.1, bf16[8,16,256,256]{3,2,1,0:T(8,128)(2,1)} %get-tuple-element.286, s32[]{:T(128)S(6)} %select_n.86), kind=kOutput, calls=%fused_computation.5.clone.1 | convolution fusion | flops 1073741824 | bytes 14680068 | tf_op jit(solution)/shard_map/while/body/eval_jaxpr/exy,esyz->esxz/dot_general | solution.py:41
  356.9 10.2 %copy.69 = f32[4,8,256,256]{3,1,2,0:T(8,128)} copy(f32[4,8,256,256]{2,3,1,0:T(8,128)} %bitcast.109) | data formatting | bytes 16777216 | tf_op jit(solution)/shard_map/while
  368.0 6.1 %fusion.45 = f32[4,256,256]{2,0,1:T(4,128)S(1)} fusion(s32[32]{0:T(128)S(1)} %broadcast_select_fusion.3, s32[4]{0:T(128)S(1)} %fusion.44, f32[4,8,256,256]{3,1,2,0:T(8,128)} %copy.69), kind=kOutput, calls=%fused_computation.2.clone.1 | convolution fusion | flops 100663424 | bytes 9437328 | tf_op jit(solution)/shard_map/while/body/eval_jaxpr/dot_general | solution.py:48
  375.8 1.8 select_reduce_fusion.2
  382.9 4.9 gather_fusion.1
  387.8 7.4 %convolution_bitcast_fusion.2 = f32[16,2,256,256]{2,3,1,0:T(8,128)} fusion(bf16[16,2,256,256]{3,2,1,0:T(8,128)(2,1)} %gather_fusion.1, bf16[8,16,256,256]{3,2,1,0:T(8,128)(2,1)} %get-tuple-element.286, s32[]{:T(128)S(6)} %select_n.86), kind=kOutput, calls=%fused_computation.5.clone.1 | convolution fusion | flops 1073741824 | bytes 14680068 | tf_op jit(solution)/shard_map/while/body/eval_jaxpr/exy,esyz->esxz/dot_general | solution.py:41
  395.2 10.2 %copy.69 = f32[4,8,256,256]{3,1,2,0:T(8,128)} copy(f32[4,8,256,256]{2,3,1,0:T(8,128)} %bitcast.109) | data formatting | bytes 16777216 | tf_op jit(solution)/shard_map/while
  406.4 6.1 %fusion.45 = f32[4,256,256]{2,0,1:T(4,128)S(1)} fusion(s32[32]{0:T(128)S(1)} %broadcast_select_fusion.3, s32[4]{0:T(128)S(1)} %fusion.44, f32[4,8,256,256]{3,1,2,0:T(8,128)} %copy.69), kind=kOutput, calls=%fused_computation.2.clone.1 | convolution fusion | flops 100663424 | bytes 9437328 | tf_op jit(solution)/shard_map/while/body/eval_jaxpr/dot_general | solution.py:48
  414.1 1.8 select_reduce_fusion.2
  421.2 5.0 gather_fusion.1
  426.3 7.4 %convolution_bitcast_fusion.2 = f32[16,2,256,256]{2,3,1,0:T(8,128)} fusion(bf16[16,2,256,256]{3,2,1,0:T(8,128)(2,1)} %gather_fusion.1, bf16[8,16,256,256]{3,2,1,0:T(8,128)(2,1)} %get-tuple-element.286, s32[]{:T(128)S(6)} %select_n.86), kind=kOutput, calls=%fused_computation.5.clone.1 | convolution fusion | flops 1073741824 | bytes 14680068 | tf_op jit(solution)/shard_map/while/body/eval_jaxpr/exy,esyz->esxz/dot_general | solution.py:41
  433.7 10.2 %copy.69 = f32[4,8,256,256]{3,1,2,0:T(8,128)} copy(f32[4,8,256,256]{2,3,1,0:T(8,128)} %bitcast.109) | data formatting | bytes 16777216 | tf_op jit(solution)/shard_map/while
  444.8 6.1 %fusion.45 = f32[4,256,256]{2,0,1:T(4,128)S(1)} fusion(s32[32]{0:T(128)S(1)} %broadcast_select_fusion.3, s32[4]{0:T(128)S(1)} %fusion.44, f32[4,8,256,256]{3,1,2,0:T(8,128)} %copy.69), kind=kOutput, calls=%fused_computation.2.clone.1 | convolution fusion | flops 100663424 | bytes 9437328 | tf_op jit(solution)/shard_map/while/body/eval_jaxpr/dot_general | solution.py:48
  452.6 1.8 select_reduce_fusion.2
  459.7 5.0 gather_fusion.1
  464.8 7.4 %convolution_bitcast_fusion.2 = f32[16,2,256,256]{2,3,1,0:T(8,128)} fusion(bf16[16,2,256,256]{3,2,1,0:T(8,128)(2,1)} %gather_fusion.1, bf16[8,16,256,256]{3,2,1,0:T(8,128)(2,1)} %get-tuple-element.286, s32[]{:T(128)S(6)} %select_n.86), kind=kOutput, calls=%fused_computation.5.clone.1 | convolution fusion | flops 1073741824 | bytes 14680068 | tf_op jit(solution)/shard_map/while/body/eval_jaxpr/exy,esyz->esxz/dot_general | solution.py:41
  472.2 10.2 %copy.69 = f32[4,8,256,256]{3,1,2,0:T(8,128)} copy(f32[4,8,256,256]{2,3,1,0:T(8,128)} %bitcast.109) | data formatting | bytes 16777216 | tf_op jit(solution)/shard_map/while
  483.3 6.1 %fusion.45 = f32[4,256,256]{2,0,1:T(4,128)S(1)} fusion(s32[32]{0:T(128)S(1)} %broadcast_select_fusion.3, s32[4]{0:T(128)S(1)} %fusion.44, f32[4,8,256,256]{3,1,2,0:T(8,128)} %copy.69), kind=kOutput, calls=%fused_computation.2.clone.1 | convolution fusion | flops 100663424 | bytes 9437328 | tf_op jit(solution)/shard_map/while/body/eval_jaxpr/dot_general | solution.py:48
  491.1 1.8 select_reduce_fusion.2
  498.2 5.3 gather_fusion.1
  503.5 7.4 %convolution_bitcast_fusion.2 = f32[16,2,256,256]{2,3,1,0:T(8,128)} fusion(bf16[16,2,256,256]{3,2,1,0:T(8,128)(2,1)} %gather_fusion.1, bf16[8,16,256,256]{3,2,1,0:T(8,128)(2,1)} %get-tuple-element.286, s32[]{:T(128)S(6)} %select_n.86), kind=kOutput, calls=%fused_computation.5.clone.1 | convolution fusion | flops 1073741824 | bytes 14680068 | tf_op jit(solution)/shard_map/while/body/eval_jaxpr/exy,esyz->esxz/dot_general | solution.py:41
  510.9 10.2 %copy.69 = f32[4,8,256,256]{3,1,2,0:T(8,128)} copy(f32[4,8,256,256]{2,3,1,0:T(8,128)} %bitcast.109) | data formatting | bytes 16777216 | tf_op jit(solution)/shard_map/while
  522.0 6.1 %fusion.45 = f32[4,256,256]{2,0,1:T(4,128)S(1)} fusion(s32[32]{0:T(128)S(1)} %broadcast_select_fusion.3, s32[4]{0:T(128)S(1)} %fusion.44, f32[4,8,256,256]{3,1,2,0:T(8,128)} %copy.69), kind=kOutput, calls=%fused_computation.2.clone.1 | convolution fusion | flops 100663424 | bytes 9437328 | tf_op jit(solution)/shard_map/while/body/eval_jaxpr/dot_general | solution.py:48
  529.8 1.8 select_reduce_fusion.2
  535.0 66.4 %psum.7 = f32[1]{0:T(128)} all-reduce(f32[1]{0:T(128)} %bitcast.26), channel_id=1, replica_groups=mesh['row'=16,'col'=8] {'row','col'}, use_global_device_ids=true, to_apply=%region_5.6 | all-reduce | flops 1 | bytes 8 | tf_op jit(solution)/shard_map/psum | solution.py:62
  (157 shorter events, 44.3 us)
Async XLA Ops:
  7.2 219.4 %all-gather.4.cloned.1.call-start = ((), (), s32[]{:S(2)}) async-start(), calls=%async_computation.1 | async-start | bytes 35651584 | tf_op jit(solution)/shard_map/all_gather | solution.py:26
  18.0 7.1 %copy-start = (s32[8,2]{0,1:T(2,128)S(1)}, s32[8,2]{0,1:T(2,128)}, u32[]{:S(2)}) copy-start(s32[8,2]{0,1:T(2,128)} %param.7) | copy-start | bytes 196
  18.0 194.6 %copy-start.1 = (s32[8,4]{0,1:T(4,128)S(1)}, s32[8,4]{0,1:T(4,128)}, u32[]{:S(2)}) copy-start(s32[8,4]{0,1:T(4,128)} %param.8) | copy-start | bytes 388
  18.0 194.7 %copy-start.2 = (s32[8]{0:T(128)S(1)}, s32[8]{0:T(128)}, u32[]{:S(2)}) copy-start(s32[8]{0:T(128)} %param.9) | copy-start | bytes 100
  18.0 194.7 %all-to-all-start = ((bf16[8,8,2,256,256]{4,3,2,1,0:T(8,128)(2,1)}), bf16[8,8,2,256,256]{4,3,2,1,0:T(8,128)(2,1)}, u32[]{:S(2)}, u32[]{:S(2)}) async-start(bf16[8,8,2,256,256]{4,3,2,1,0:T(8,128)(2,1)} %stack.2), calls=%async_computation | async-start | bytes 33554432 | tf_op jit(solution)/shard_map/all_to_all | solution.py:9
Sparse Core Ops, SparseCore 0:
  11.3 199.8 all-gather.3
